TPU v7x, 32 devices: a whole 2x2x4 slice. The times are simulated.
32 devices in a mesh: dp: 16 (over z, x, core), mp: 2 (over y).
Axes of the slice: x: 2, y: 2, z: 4, core: 2. Of those that a mesh axis runs over, the one named last changes fastest.
Arguments:
- tokens: bfloat16 [16384, 1024], P('dp'), may hold values from -6 to 6
- page_lengths: int32 [32], P('dp'), may hold values from 64 to 512, as said below
- qkv_weight: bfloat16 [3, 1024, 1024], P(None, None, 'mp'), may hold values from -0.1875 to 0.1875
- qv_bias: bfloat16 [2, 1024], P(None, 'mp'), may hold values from -1.5 to 1.5
- out_weight: bfloat16 [1024, 1024], P('mp'), may hold values from -0.75 to 0.75
- out_bias: bfloat16 [1024], replicated, may hold values from -1.5 to 1.5
- ln1_gain: bfloat16 [1024], replicated, may hold values from 0.5 to 1.5
- ln1_bias: bfloat16 [1024], replicated, may hold values from -1.5 to 1.5
- ff1_weight: bfloat16 [1024, 4096], P(None, 'mp'), may hold values from -0.1875 to 0.1875
- ff1_bias: bfloat16 [4096], P('mp'), may hold values from -1.5 to 1.5
- ff2_weight: bfloat16 [4096, 1024], P('mp'), may hold values from -0.09375 to 0.09375
- ff2_bias: bfloat16 [1024], replicated, may hold values from -1.5 to 1.5
- ln2_gain: bfloat16 [1024], replicated, may hold values from 0.5 to 1.5
- ln2_bias: bfloat16 [1024], replicated, may hold values from -1.5 to 1.5
- cotangent: bfloat16 [16384, 1024], P('dp'), may hold values from -6 to 6
Outputs:
- out_rows: bfloat16 [16384, 1024], P(('dp', 'mp'))
- input_grad: bfloat16 [16384, 1024], P(('dp', 'mp'))
- qkv_weight_grad: float32 [3, 1024, 1024], P(None, 'dp', 'mp')
- qv_bias_grad: float32 [2, 1024], replicated
- out_weight_grad: float32 [1024, 1024], P('mp', 'dp')
- out_bias_grad: float32 [1024], replicated
- ln1_gain_grad: float32 [1024], replicated
- ln1_bias_grad: float32 [1024], replicated
- ff1_weight_grad: float32 [1024, 4096], P('dp', 'mp')
- ff1_bias_grad: float32 [4096], replicated
- ff2_weight_grad: float32 [4096, 1024], P('mp', 'dp')
- ff2_bias_grad: float32 [1024], replicated
- ln2_gain_grad: float32 [1024], replicated
- ln2_bias_grad: float32 [1024], replicated
Inputs may be any that keep to these rules, and one draw needn't show every extreme that they name: `page_lengths`: valid tokens of a page; some page has all 512 slots valid.
All inputs are finite; a program needn't handle non-finite values.
Results may differ from a plain program's by a relative error of at most 0.02.
Values may be sent and summed in bfloat16 or wider, within the bound.
No kernel may reach another device: no remote copies, remote signals or barrier semaphores. Data moves between devices by JAX's collectives and lax.ppermute only.
A program may use at most 192 MiB of HBM per device.

v0:
```python
import jax
import jax.numpy as jnp
from jax import lax
from jax.sharding import PartitionSpec as P

HD = 64
EPSILON = 1e-05
NEGATIVE = -1e30


def normalize(values):
    center = values - jnp.mean(values, axis=-1, keepdims=True)
    spread = jnp.mean(center * center, axis=-1, keepdims=True)
    return center * lax.rsqrt(spread + EPSILON)


def gelu_exact(values):
    return jax.nn.gelu(values, approximate=False)


def over_rows(left, right):
    return lax.dot_general(
        left, right, (((0,), (0,)), ((), ())), preferred_element_type=jnp.float32
    )


def over_cols(left, right):
    return lax.dot_general(
        left, right, (((1,), (1,)), ((), ())), preferred_element_type=jnp.float32
    )


def page_scores(query, keyset, valid):
    raw = jnp.einsum("qhe,khe->hqk", query, keyset, preferred_element_type=jnp.float32) * HD ** (
        -0.5
    )
    return jnp.where(valid[None, None, :], raw, NEGATIVE)


def attend(block):
    query, keyset, valueset, valid = block
    scores = page_scores(query, keyset, valid)
    top = jnp.max(scores, axis=-1, keepdims=True)
    expo = jnp.exp(scores - top)
    total = jnp.sum(expo, axis=-1, keepdims=True)
    probs = expo / total
    context = jnp.einsum(
        "hqk,khe->qhe", probs.astype(jnp.bfloat16), valueset, preferred_element_type=jnp.float32
    )
    context = context.astype(jnp.bfloat16)
    return (context.reshape(context.shape[0], -1), top[..., 0] + jnp.log(total[..., 0]))


def attend_back(block):
    query, keyset, valueset, valid, logsum, dcontext = block
    scale = HD ** (-0.5)
    scores = page_scores(query, keyset, valid)
    probs = jnp.exp(scores - logsum[..., None])
    dprobs = jnp.einsum("qhe,khe->hqk", dcontext, valueset, preferred_element_type=jnp.float32)
    delta = jnp.sum(probs * dprobs, axis=-1, keepdims=True)
    dscores = (probs * (dprobs - delta)).astype(jnp.bfloat16)
    dquery = (
        jnp.einsum("hqk,khe->qhe", dscores, keyset, preferred_element_type=jnp.float32) * scale
    ).astype(jnp.bfloat16)
    dkeys = (
        jnp.einsum("hqk,qhe->khe", dscores, query, preferred_element_type=jnp.float32) * scale
    ).astype(jnp.bfloat16)
    dvalues = jnp.einsum(
        "hqk,qhe->khe", probs.astype(jnp.bfloat16), dcontext, preferred_element_type=jnp.float32
    ).astype(jnp.bfloat16)
    seq_len = query.shape[0]
    return (dquery.reshape(seq_len, -1), dkeys.reshape(seq_len, -1), dvalues.reshape(seq_len, -1))


def local(
    tokens,
    page_lengths,
    qkv_weight,
    qv_bias,
    out_weight,
    out_bias,
    ln1_gain,
    ln1_bias,
    ff1_weight,
    ff1_bias,
    ff2_weight,
    ff2_bias,
    ln2_gain,
    ln2_bias,
    cotangent,
):
    row_count = tokens.shape[0]
    page_count = page_lengths.shape[0]
    seq_len = row_count // page_count
    cols = qkv_weight.shape[2]
    ff_cols = ff1_weight.shape[1]
    group_heads = cols // HD
    share = row_count // lax.axis_size("mp")
    group = lax.axis_index("mp")
    share_start = group * share
    gain_one = ln1_gain.astype(jnp.float32)
    shift_one = ln1_bias.astype(jnp.float32)
    gain_two = ln2_gain.astype(jnp.float32)
    shift_two = ln2_bias.astype(jnp.float32)

    def own_rows(values):
        return lax.dynamic_slice_in_dim(values, share_start, share, 0)

    projected = jnp.einsum("rd,tdc->trc", tokens, qkv_weight, preferred_element_type=jnp.float32)
    bias_rows = jnp.stack([qv_bias[0], jnp.zeros_like(qv_bias[0]), qv_bias[1]]).astype(jnp.float32)
    qkv_rows = (projected + bias_rows[:, None, :]).astype(jnp.bfloat16)
    qkv_pages = qkv_rows.reshape(3, page_count, seq_len, group_heads, HD)
    valid = jnp.arange(seq_len)[None, :] < page_lengths[:, None]
    context, logsum = lax.map(attend, (qkv_pages[0], qkv_pages[1], qkv_pages[2], valid))
    context = context.reshape(row_count, cols)
    attn_part = jnp.dot(context, out_weight, preferred_element_type=jnp.float32).astype(
        jnp.bfloat16
    )
    attn = lax.psum(attn_part, "mp").astype(jnp.float32)
    first_sum = tokens.astype(jnp.float32) + attn + out_bias.astype(jnp.float32)
    normed_one, norm_one_back = jax.vjp(normalize, first_sum)
    hidden = normed_one * gain_one + shift_one
    hidden_low = hidden.astype(jnp.bfloat16)
    normed_one_own = own_rows(normed_one)
    pre = jnp.dot(hidden_low, ff1_weight, preferred_element_type=jnp.float32) + ff1_bias.astype(
        jnp.float32
    )
    activated, gelu_back = jax.vjp(gelu_exact, pre)
    act_low = activated.astype(jnp.bfloat16)
    ffn_part = jnp.dot(act_low, ff2_weight, preferred_element_type=jnp.float32).astype(jnp.bfloat16)
    cot_own = own_rows(cotangent).astype(jnp.float32)
    ffn = lax.psum(ffn_part, "mp").astype(jnp.float32)
    second_sum = hidden + ffn + ff2_bias.astype(jnp.float32)
    normed_two, norm_two_back = jax.vjp(normalize, second_sum)
    normed_two_own = own_rows(normed_two)
    out_rows = (normed_two_own * gain_two + shift_two).astype(jnp.bfloat16)
    dsecond = norm_two_back(cotangent.astype(jnp.float32) * gain_two)[0]
    dffn = dsecond.astype(jnp.bfloat16)
    dsecond_own = own_rows(dsecond)
    dgain_two = jnp.sum(cot_own * normed_two_own, axis=0)
    dshift_two = jnp.sum(cot_own, axis=0)
    dff2_bias = jnp.sum(dsecond_own, axis=0)
    dff2_weight = over_rows(act_low, dffn)
    dact = over_cols(dffn, ff2_weight)
    dpre = gelu_back(dact)[0].astype(jnp.bfloat16)
    dff1_bias = jnp.sum(dpre.astype(jnp.float32), axis=0)
    dff1_weight = over_rows(hidden_low, dpre)
    dhid_part = over_cols(dpre, ff1_weight).astype(jnp.bfloat16)
    dhidden = dsecond + lax.psum(dhid_part, "mp").astype(jnp.float32)
    dfirst = norm_one_back(dhidden * gain_one)[0]
    dattn = dfirst.astype(jnp.bfloat16)
    dhidden_own = own_rows(dhidden)
    dfirst_own = own_rows(dfirst)
    dgain_one = jnp.sum(dhidden_own * normed_one_own, axis=0)
    dshift_one = jnp.sum(dhidden_own, axis=0)
    dout_bias = jnp.sum(dfirst_own, axis=0)
    dout_weight = over_rows(context, dattn)
    dcontext = over_cols(dattn, out_weight).astype(jnp.bfloat16)
    dcontext_pages = dcontext.reshape(page_count, seq_len, group_heads, HD)
    dquery, dkeys, dvalues = lax.map(
        attend_back, (qkv_pages[0], qkv_pages[1], qkv_pages[2], valid, logsum, dcontext_pages)
    )
    dqkv = jnp.stack(
        [
            dquery.reshape(row_count, cols),
            dkeys.reshape(row_count, cols),
            dvalues.reshape(row_count, cols),
        ]
    )
    dqv_bias = jnp.stack(
        [jnp.sum(dqkv[0].astype(jnp.float32), axis=0), jnp.sum(dqkv[2].astype(jnp.float32), axis=0)]
    )
    dqkv_weight = jnp.einsum("rd,trc->tdc", tokens, dqkv, preferred_element_type=jnp.float32)
    dtok_part = jnp.einsum(
        "trc,tdc->rd", dqkv, qkv_weight, preferred_element_type=jnp.float32
    ).astype(jnp.bfloat16)
    input_grad = (
        dfirst_own
        + lax.psum_scatter(dtok_part, "mp", scatter_dimension=0, tiled=True).astype(jnp.float32)
    ).astype(jnp.bfloat16)
    qkv_share, out_share, ff1_share, ff2_share = (
        lax.psum_scatter(
            dqkv_weight.astype(jnp.bfloat16), "dp", scatter_dimension=1, tiled=True
        ).astype(jnp.float32),
        lax.psum_scatter(
            dout_weight.astype(jnp.bfloat16), "dp", scatter_dimension=1, tiled=True
        ).astype(jnp.float32),
        lax.psum_scatter(
            dff1_weight.astype(jnp.bfloat16), "dp", scatter_dimension=0, tiled=True
        ).astype(jnp.float32),
        lax.psum_scatter(
            dff2_weight.astype(jnp.bfloat16), "dp", scatter_dimension=1, tiled=True
        ).astype(jnp.float32),
    )
    qv_placed = lax.dynamic_update_slice_in_dim(
        jnp.zeros((2, cols * lax.axis_size("mp")), jnp.float32), dqv_bias, group * cols, 1
    )
    ff1_placed = lax.dynamic_update_slice_in_dim(
        jnp.zeros((ff_cols * lax.axis_size("mp"),), jnp.float32), dff1_bias, group * ff_cols, 0
    )
    small = lax.psum(
        (qv_placed, dout_bias, dgain_one, dshift_one, ff1_placed, dff2_bias, dgain_two, dshift_two),
        ("dp", "mp"),
    )
    return (
        out_rows,
        input_grad,
        qkv_share,
        small[0],
        out_share,
        small[1],
        small[2],
        small[3],
        ff1_share,
        small[4],
        ff2_share,
        small[5],
        small[6],
        small[7],
    )


def solution(mesh):
    in_specs = (
        P("dp", None),
        P("dp"),
        P(None, None, "mp"),
        P(None, "mp"),
        P("mp", None),
        P(),
        P(),
        P(),
        P(None, "mp"),
        P("mp"),
        P("mp", None),
        P(),
        P(),
        P(),
        P("dp", None),
    )
    out_specs = (
        P(("dp", "mp"), None),
        P(("dp", "mp"), None),
        P(None, "dp", "mp"),
        P(),
        P("mp", "dp"),
        P(),
        P(),
        P(),
        P("dp", "mp"),
        P(),
        P("mp", "dp"),
        P(),
        P(),
        P(),
    )
    return jax.shard_map(local, mesh=mesh, in_specs=in_specs, out_specs=out_specs, check_vma=False)
```

profile of v0, /device:TPU:0, one launch (start us, length us, event | category | flops | bytes accessed | tf_op | source)
XLA Modules:
  0.0 775.8 jit_solution(8002461027185806768)
XLA Ops:
  9.1 5.5 fusion.56
  16.3 2.6 squeeze.41
  18.9 2.4 copy.72
  21.4 2.6 squeeze.40
  24.0 2.4 copy.71
  26.4 2.6 squeeze.39
  32.4 24.3 %while.26 = (s32[]{:T(128)}, bf16[2,512,512]{2,1,0:T(8,128)(2,1)}, f32[2,8,512]{2,1,0:T(8,128)S(1)}, bf16[2,512,8,64]{1,3,2,0:T(8,128)(2,1)}, pred[2,512]{1,0:T(...) while((s32[]{:T(128)}, bf16[2,512,512]{2,1,0:T(8,128)(2,1)}, ...), condition=%wide.region_3.4_spmd, body=%wide.region_0.3_spmd.sunk | while | flops 562294784 | bytes 33689224 | solution.py:114
  32.5 3.1 fusion.115
  37.6 3.0 fusion.117
  44.6 3.1 fusion.115
  49.8 3.0 fusion.117
  56.7 4.2 convolution_convert_fusion.4
  61.3 65.4 %all-reduce.7.cloned.1.call-done = bf16[1024,1024]{1,0:T(8,128)(2,1)} async-done(((bf16[1024,1024]{1,0:T(8,128)(2,1)}), bf16[1024,1024]{1,0:T(8,128)(2,1)}) %all-reduce.7.cloned.1.call-update) | async-done | bytes 2097168 | tf_op jit(solution)/shard_map/psum | solution.py:119
  126.7 3.1 fusion.54
  133.5 24.4 %multiply_convert_fusion.1 = (bf16[1024,2048]{1,0:T(8,128)(2,1)S(1)}, f32[1024,2048]{1,0:T(8,128)}, f32[1024,2048]{1,0:T(8,128)}) fusion(f32[2048]{0:T(1024)S(1)} %convert_element_type.172, bf16[1024,2048]{1,0:T(8,128)(2,1)S(1)} %copy-done.36, f32[1024,1024]{1,0:T(8,128)S(1)} %broadcast_multiply_fusion, f32[1024]{0:T(1024)S(1)} %convert_element_type.170, ...), kind=kOutput, calls=%fused_computation.64 | convolution fusion | flops 4436525056 | bytes 29376512 | tf_op jit(solution)/shard_map/dot_general | solution.py:125
  159.9 5.7 convolution_convert_fusion.3
  166.2 62.6 %all-reduce.9.cloned.1.call-done = bf16[1024,1024]{1,0:T(8,128)(2,1)} async-done(((bf16[1024,1024]{1,0:T(8,128)(2,1)}), bf16[1024,1024]{1,0:T(8,128)(2,1)}) %all-reduce.9.cloned.1.call-update) | async-done | bytes 2097168 | tf_op jit(solution)/shard_map/psum | solution.py:132
  228.8 3.9 fusion.58
  233.5 3.5 multiply_reduce_fusion.2
  241.1 13.0 %convert_reduce_fusion = (f32[2048]{0:T(1024)}, bf16[1024,2048]{1,0:T(8,128)(2,1)}) fusion(f32[1024,2048]{1,0:T(8,128)} %get-tuple-element.258, bf16[2048,1024]{1,0:T(8,128)(2,1)S(1)} %copy-done.35, f32[1024,1024]{1,0:T(8,128)S(1)} %broadcast_add_fusion.1, f32[1024,2048]{1,0:T(8,128)} %get-tuple-element.275, f32[2048]{0:T(1024)S(1)} %convert_element_type.172), kind=kOutput, calls=%fused_computation.62 | convolution fusion | flops 4331665408 | bytes 29376512 | tf_op jit(solution)/shard_map/dot_general | solution.py:28
  254.1 8.0 %convolution_convert_fusion.2 = bf16[1024,1024]{1,0:T(8,128)(2,1)} fusion(bf16[1024,2048]{1,0:T(8,128)(2,1)} %get-tuple-element.277, bf16[1024,2048]{1,0:T(8,128)(2,1)S(1)} %copy-done.37), kind=kOutput, calls=%fused_computation.118 | convolution fusion | flops 4296015872 | bytes 10485760 | tf_op jit(solution)/shard_map/dot_general | solution.py:28
  262.2 63.0 %all-reduce.11.cloned.1.call-done = bf16[1024,1024]{1,0:T(8,128)(2,1)} async-done(((bf16[1024,1024]{1,0:T(8,128)(2,1)}), bf16[1024,1024]{1,0:T(8,128)(2,1)}) %all-reduce.11.cloned.1.call-update) | async-done | bytes 2097168 | tf_op jit(solution)/shard_map/psum | solution.py:149
  325.2 5.7 multiply_reduce_fusion.1
  337.9 3.9 reshape.153
  341.8 3.3 copy.77
  346.2 42.9 %while.27 = (s32[]{:T(128)}, bf16[2,512,512]{1,2,0:T(8,128)(2,1)}, bf16[2,512,512]{2,1,0:T(8,128)(2,1)}, bf16[2,512,512]{1,2,0:T(8,128)(2,1)}, bf16[2,512,8,64]{...) while((s32[]{:T(128)}, bf16[2,512,512]{1,2,0:T(8,128)(2,1)}, ...), condition=%wide.region_17.18_spmd, body=%wide.region_15.17_spmd.sunk | while | flops 1374941184 | bytes 89248512 | solution.py:160
  346.2 2.6 fusion.126
  348.8 2.9 fusion.127
  351.8 3.0 multiply_reduce_fusion.7
  354.7 2.8 multiply_convert_fusion.3
  367.6 2.6 fusion.126
  370.2 2.9 fusion.127
  373.1 3.0 multiply_reduce_fusion.7
  376.1 2.8 multiply_convert_fusion.3
  393.7 7.7 convert_bitcast_fusion
  401.4 7.7 copy.83
  409.1 4.8 convolution_convert_fusion.5
  414.0 10.2 %convolution_convert_fusion = bf16[2048,1024]{0,1:T(8,128)(2,1)} fusion(bf16[1024,2048]{1,0:T(8,128)(2,1)} %copy-done.40, f32[1024,1024]{1,0:T(8,128)} %copy-done.11), kind=kOutput, calls=%fused_computation.91 | convolution fusion | flops 4298113024 | bytes 12582912 | tf_op jit(solution)/shard_map/dot_general | solution.py:22
  424.3 6.6 bitcast_convert_fusion
  431.3 10.2 %convolution_convert_fusion.1 = bf16[1024,2048]{1,0:T(8,128)(2,1)} fusion(bf16[1024,2048]{1,0:T(8,128)(2,1)} %get-tuple-element.277, f32[1024,1024]{1,0:T(8,128)} %copy-done.7, f32[1024]{0:T(1024)S(1)} %copy-done.25, f32[1024]{0:T(1024)S(1)} %convert_element_type.169), kind=kOutput, calls=%fused_computation.92 | convolution fusion | flops 4300210176 | bytes 12591104 | tf_op jit(solution)/shard_map/dot_general | solution.py:22
  445.8 3.6 convert_reduce_fusion.1
  452.0 68.8 %all-reduce.13.cloned.1.call-done = bf16[3,1024,512]{2,0,1:T(4,128)(2,1)} async-done(((bf16[3,1024,512]{2,0,1:T(4,128)(2,1)}), bf16[3,1024,512]{2,0,1:T(4,128)(2,1)}) %all-reduce.13.cloned.1.call-update) | async-done | bytes 3145744
  522.7 57.9 %reduce-scatter.7.cloned.1.call-done = bf16[512,64]{0,1:T(8,128)(2,1)} async-done(((bf16[512,1024]{0,1:T(8,128)(2,1)}), bf16[512,64]{0,1:T(8,128)(2,1)}) %reduce-scatter.7.cloned.1.call-update) | async-done | bytes 65552 | tf_op jit(solution)/shard_map/reduce_scatter | solution.py:185
  582.1 74.2 %reduce-scatter.11.cloned.1.call-done = bf16[2048,64]{0,1:T(8,128)(2,1)} async-done(((bf16[2048,1024]{0,1:T(8,128)(2,1)}), bf16[2048,64]{0,1:T(8,128)(2,1)}) %reduce-scatter.11.cloned.1.call-update) | async-done | bytes 262160 | tf_op jit(solution)/shard_map/reduce_scatter | solution.py:191
  658.1 31.3 %reduce-scatter.5.cloned.1.call-done = bf16[512,1024]{1,0:T(8,128)(2,1)} async-done(((bf16[1024,1024]{1,0:T(8,128)(2,1)}), bf16[512,1024]{1,0:T(8,128)(2,1)}) %reduce-scatter.5.cloned.1.call-update) | async-done | bytes 1048592 | tf_op jit(solution)/shard_map/reduce_scatter | solution.py:179
  689.4 3.2 dynamic-slice_reduce_fusion.4
  692.6 40.9 %all-reduce.1 = (f32[2,1024]{1,0:T(2,128)}, f32[1024]{0:T(1024)}, f32[1024]{0:T(1024)}, f32[1024]{0:T(1024)}, f32[4096]{0:T(1024)}, /*index=5*/f32[1024]{0:T(1024)}, f32[1024]{0:T(1024)}, f32[1024]{0:T(1024)}) all-reduce(f32[2,1024]{1,0:T(2,128)S(1)} %maximum_dynamic-update-slice_fusion, ...), channel_id=1, replica_groups=mesh['dp'=16,'mp'=2] {'dp','mp'}, use_global_device_ids=true, to_apply=%region_22.23 | all-reduce | flops 12288 | bytes 98304 | tf_op jit(solution)/shard_map/psum | solution.py:201
  733.5 33.2 %reduce-scatter.9.cloned.1.call-done = bf16[64,2048]{1,0:T(8,128)(2,1)} async-done(((bf16[1024,2048]{1,0:T(8,128)(2,1)}), bf16[64,2048]{1,0:T(8,128)(2,1)}) %reduce-scatter.9.cloned.1.call-update) | async-done | bytes 262160 | tf_op jit(solution)/shard_map/reduce_scatter | solution.py:188
  (180 shorter events, 76.3 us)
Async XLA Ops:
  7.2 119.5 %all-reduce.7.cloned.1.call-start = ((), (), s32[]{:S(2)}) async-start(), calls=%async_computation.4 | async-start | bytes 4194304 | tf_op jit(solution)/shard_map/psum | solution.py:119
  35.6 2.0 copy-start.15
  56.7 4.5 copy-start.28
  56.7 4.5 copy-start.29
  56.7 4.5 copy-start.30
  56.7 4.6 copy-start.27
  60.9 167.8 %all-reduce.9.cloned.1.call-start = ((), (), s32[]{:S(2)}) async-start(), calls=%async_computation.5 | async-start | bytes 4194304 | tf_op jit(solution)/shard_map/psum | solution.py:132
  61.3 171.4 %copy-start.24 = (f32[1024]{0:T(1024)}, f32[1024]{0:T(1024)S(1)}, u32[]{:S(2)}) copy-start(f32[1024]{0:T(1024)S(1)} %convert_element_type.170) | copy-start | bytes 12292
  126.7 3.1 copy-start.3
  126.7 3.5 copy-start.5
  131.3 2.2 copy-start.36
  133.4 24.4 %copy-start.7 = (f32[1024,1024]{1,0:T(8,128)}, f32[1024,1024]{1,0:T(8,128)S(1)}, u32[]{:S(2)}) copy-start(f32[1024,1024]{1,0:T(8,128)S(1)} %broadcast_multiply_fusion) | copy-start | bytes 12582916
  133.5 26.5 %copy-start.34 = (bf16[2048,1024]{1,0:T(8,128)(2,1)S(1)}, bf16[2048,1024]{1,0:T(8,128)(2,1)}, u32[]{:S(2)}) copy-start(bf16[2048,1024]{1,0:T(8,128)(2,1)} %param.29) | copy-start | bytes 12582916
  157.9 2.0 copy-start.40
  159.9 6.2 copy-start.31
  159.9 6.2 copy-start.32
  165.7 159.5 %all-reduce.11.cloned.1.call-start = ((), (), s32[]{:S(2)}) async-start(), calls=%async_computation.6 | async-start | bytes 4194304 | tf_op jit(solution)/shard_map/psum | solution.py:149
  166.2 72.0 %copy-start.20 = (f32[1024]{0:T(1024)}, f32[1024]{0:T(1024)S(1)}, u32[]{:S(2)}) copy-start(f32[1024]{0:T(1024)S(1)} %convert_element_type.177) | copy-start | bytes 12292
  228.8 4.0 copy-start.8
  228.8 4.7 copy-start.13
  237.0 2.4 copy-start.10
  237.0 2.4 copy-start.22
  238.2 3.0 copy-start.35
  239.4 14.7 %copy-start.11 = (f32[1024,1024]{1,0:T(8,128)}, f32[1024,1024]{1,0:T(8,128)S(1)}, u32[]{:S(2)}) copy-start(f32[1024,1024]{1,0:T(8,128)S(1)} %broadcast_add_fusion.1) | copy-start | bytes 12582916
  241.1 13.0 %copy-start.37 = (bf16[1024,2048]{1,0:T(8,128)(2,1)S(1)}, bf16[1024,2048]{1,0:T(8,128)(2,1)}, u32[]{:S(2)}) copy-start(bf16[1024,2048]{1,0:T(8,128)(2,1)} %param.27) | copy-start | bytes 12582916
  262.1 258.7 %all-reduce.13.cloned.1.call-start = ((), (), s32[]{:S(2)}) async-start(), calls=%async_computation.11 | async-start | bytes 8388608
  325.2 5.8 copy-start.4
  325.2 5.8 copy-start.6
  330.9 2.4 copy-start.12
  333.4 2.3 copy-start.38
  346.2 2.6 copy-start.14
  348.8 2.9 copy-start.16
  354.7 2.9 copy-start.2
  357.6 2.2 copy-start.1
  367.6 2.6 copy-start.14
  370.2 2.9 copy-start.16
  376.1 2.9 copy-start.2
  379.0 2.2 copy-start.1
  409.1 171.5 %reduce-scatter.7.cloned.1.call-start = ((), (), s32[]{:S(2)}) async-start(), calls=%async_computation.8 | async-start | bytes 1114112 | tf_op jit(solution)/shard_map/reduce_scatter | solution.py:185
  414.0 242.3 %reduce-scatter.11.cloned.1.call-start = ((), (), s32[]{:S(2)}) async-start(), calls=%async_computation.10 | async-start | bytes 4456448 | tf_op jit(solution)/shard_map/reduce_scatter | solution.py:191
  424.3 7.0 copy-start.25
  424.3 265.1 %reduce-scatter.5.cloned.1.call-start = ((), (), s32[]{:S(2)}) async-start(), calls=%async_computation.7 | async-start | bytes 3145728 | tf_op jit(solution)/shard_map/reduce_scatter | solution.py:179
  431.0 335.8 %reduce-scatter.9.cloned.1.call-start = ((), (), s32[]{:S(2)}) async-start(), calls=%async_computation.9 | async-start | bytes 4456448 | tf_op jit(solution)/shard_map/reduce_scatter | solution.py:188
  441.5 2.0 copy-start.26
  441.5 4.3 copy-start.21
  443.4 6.0 copy-start.9
  445.8 5.8 copy-start.18
  445.8 5.8 copy-start.19
  (6 other events, 9.1 us)
Sparse Core Ops, SparseCore 0:
  61.1 65.5 all-reduce.6
  165.8 62.9 all-reduce.8
  262.2 62.9 all-reduce.10
  409.2 111.5 all-reduce.12
  524.3 56.2 reduce-scatter.6
  584.8 71.4 reduce-scatter.10
  658.5 30.8 reduce-scatter.4
  693.8 72.9 reduce-scatter.8
where the time goes:
time: 785 us; the launch traced here: 776 us
  waiting for transfers between devices  457 us (58%)
  matrix products  139 us (18%)
  local copies, waits for them, and re-layouts  70.2 us (9%)
  other arithmetic  51.3 us (7%)
  blocking collectives  40.9 us (5%)
  between operations  15.7 us (2%)
    reduce_scatter x1, waiting for transfers between devices, local(): lax.psum_scatter(dff2_weight.astype(jnp.bfloat16), 'dp', scatter_dimensio...  74.2 us
    unnamed x9, waiting for transfers between devices  68.9 us
    psum x1, waiting for transfers between devices, local(): attn = lax.psum(attn_part, 'mp').astype(jnp.float32)  65.4 us
    psum x1, waiting for transfers between devices, local(): dhidden = dsecond + lax.psum(dhid_part, 'mp').astype(jnp.float32)  63 us
    psum x1, waiting for transfers between devices, local(): ffn = lax.psum(ffn_part, 'mp').astype(jnp.float32)  62.6 us
    reduce_scatter x1, waiting for transfers between devices, local(): lax.psum_scatter(dout_weight.astype(jnp.bfloat16), 'dp', scatter_dimensio...  57.9 us
    psum x1, blocking collectives, local(): lax.psum((qv_placed, dout_bias, dgain_one, dshift_one, ff1_placed, dff2_b...  40.9 us
    reduce_scatter x1, waiting for transfers between devices, local(): lax.psum_scatter(dff1_weight.astype(jnp.bfloat16), 'dp', scatter_dimensio...  33.2 us
  transfers between devices with their start and end apart: 8, of which 8 were waited for; matrix products, arithmetic and copies ran while one was open for 6% of the time, Pallas kernels for 0%

commit v1 on v0

--- a/solution.py
+++ b/solution.py
@@ -199,8 +199,20 @@
         jnp.zeros((ff_cols * lax.axis_size("mp"),), jnp.float32), dff1_bias, group * ff_cols, 0
     )
     small = lax.psum(
-        (qv_placed, dout_bias, dgain_one, dshift_one, ff1_placed, dff2_bias, dgain_two, dshift_two),
-        ("dp", "mp"),
+        lax.psum(
+            (
+                qv_placed,
+                dout_bias,
+                dgain_one,
+                dshift_one,
+                ff1_placed,
+                dff2_bias,
+                dgain_two,
+                dshift_two,
+            ),
+            "dp",
+        ),
+        "mp",
     )
     return (
         out_rows,

time: 785 us -> 785 us (level)
  waiting for transfers between devices: 457 us -> 427 us
  blocking collectives: 40.9 us -> 70.6 us
    reduce_scatter x1, waiting for transfers between devices: 33.2 us -> 3.53 us  [local(): lax.psum_scatter(dff1_weight.astype(jnp.bfloat16), 'dp', scatter_dimensio...]
    psum x1, blocking collectives: 40.9 us -> 62.3 us  [local(): lax.psum((qv_placed, dout_bias, dgain_one, dshift_one, ff1_placed, dff2_b...]
    psum x0 -> x1, blocking collectives: none -> 8.3 us  [local(): lax.psum(lax.psum((qv_placed, dout_bias, dgain_one, dshift_one, ff1_place...]
where the time goes in v1:
time: 785 us; the launch traced here: 776 us
  waiting for transfers between devices  427 us (54%)
  matrix products  139 us (18%)
  blocking collectives  70.6 us (9%)
  local copies, waits for them, and re-layouts  70.2 us (9%)
  other arithmetic  51.3 us (7%)
  between operations  15.7 us (2%)
    reduce_scatter x1, waiting for transfers between devices, local(): lax.psum_scatter(dff2_weight.astype(jnp.bfloat16), 'dp', scatter_dimensio...  74.2 us
    unnamed x9, waiting for transfers between devices  68.9 us
    psum x1, waiting for transfers between devices, local(): attn = lax.psum(attn_part, 'mp').astype(jnp.float32)  65.4 us
    psum x1, waiting for transfers between devices, local(): dhidden = dsecond + lax.psum(dhid_part, 'mp').astype(jnp.float32)  63 us
    psum x1, waiting for transfers between devices, local(): ffn = lax.psum(ffn_part, 'mp').astype(jnp.float32)  62.6 us
    psum x1, blocking collectives, local(): lax.psum((qv_placed, dout_bias, dgain_one, dshift_one, ff1_placed, dff2_b...  62.3 us
    reduce_scatter x1, waiting for transfers between devices, local(): lax.psum_scatter(dout_weight.astype(jnp.bfloat16), 'dp', scatter_dimensio...  57.9 us
    reduce_scatter x1, waiting for transfers between devices, local(): lax.psum_scatter(dtok_part, 'mp', scatter_dimension=0, tiled=True)  31.3 us
  transfers between devices with their start and end apart: 8, of which 8 were waited for; matrix products, arithmetic and copies ran while one was open for 6% of the time, Pallas kernels for 0%

profile of v1, /device:TPU:0, one launch (start us, length us, event | category | flops | bytes accessed | tf_op | source)
XLA Modules:
  0.0 775.8 jit_solution(8641743296553900225)
XLA Ops:
  9.1 5.5 fusion.56
  16.3 2.6 squeeze.41
  18.9 2.4 copy.72
  21.4 2.6 squeeze.40
  26.4 2.6 squeeze.39
  32.4 24.3 %while.26 = (s32[]{:T(128)}, bf16[2,512,512]{2,1,0:T(8,128)(2,1)}, f32[2,8,512]{2,1,0:T(8,128)S(1)}, bf16[2,512,8,64]{1,3,2,0:T(8,128)(2,1)}, pred[2,512]{1,0:T(...) while((s32[]{:T(128)}, bf16[2,512,512]{2,1,0:T(8,128)(2,1)}, ...), condition=%wide.region_3.4_spmd, body=%wide.region_0.3_spmd.sunk | while | flops 562294784 | bytes 33689224 | solution.py:114
  32.5 3.1 fusion.115
  37.6 3.0 fusion.117
  44.6 3.1 fusion.115
  49.8 3.0 fusion.117
  56.7 4.2 convolution_convert_fusion.4
  61.3 65.4 %all-reduce.8.cloned.1.call-done = bf16[1024,1024]{1,0:T(8,128)(2,1)} async-done(((bf16[1024,1024]{1,0:T(8,128)(2,1)}), bf16[1024,1024]{1,0:T(8,128)(2,1)}) %all-reduce.8.cloned.1.call-update) | async-done | bytes 2097168 | tf_op jit(solution)/shard_map/psum | solution.py:119
  126.7 3.1 fusion.54
  133.5 24.4 %multiply_convert_fusion.1 = (bf16[1024,2048]{1,0:T(8,128)(2,1)S(1)}, f32[1024,2048]{1,0:T(8,128)}, f32[1024,2048]{1,0:T(8,128)}) fusion(f32[2048]{0:T(1024)S(1)} %convert_element_type.172, bf16[1024,2048]{1,0:T(8,128)(2,1)S(1)} %copy-done.36, f32[1024,1024]{1,0:T(8,128)S(1)} %broadcast_multiply_fusion, f32[1024]{0:T(1024)S(1)} %convert_element_type.170, ...), kind=kOutput, calls=%fused_computation.64 | convolution fusion | flops 4436525056 | bytes 29376512 | tf_op jit(solution)/shard_map/dot_general | solution.py:125
  159.9 5.7 convolution_convert_fusion.3
  166.2 62.6 %all-reduce.10.cloned.1.call-done = bf16[1024,1024]{1,0:T(8,128)(2,1)} async-done(((bf16[1024,1024]{1,0:T(8,128)(2,1)}), bf16[1024,1024]{1,0:T(8,128)(2,1)}) %all-reduce.10.cloned.1.call-update) | async-done | bytes 2097168 | tf_op jit(solution)/shard_map/psum | solution.py:132
  228.8 3.9 fusion.58
  233.5 3.5 multiply_reduce_fusion.2
  241.1 13.0 %convert_reduce_fusion = (f32[2048]{0:T(1024)}, bf16[1024,2048]{1,0:T(8,128)(2,1)}) fusion(f32[1024,2048]{1,0:T(8,128)} %get-tuple-element.266, bf16[2048,1024]{1,0:T(8,128)(2,1)S(1)} %copy-done.35, f32[1024,1024]{1,0:T(8,128)S(1)} %broadcast_add_fusion.1, f32[1024,2048]{1,0:T(8,128)} %get-tuple-element.283, f32[2048]{0:T(1024)S(1)} %convert_element_type.172), kind=kOutput, calls=%fused_computation.62 | convolution fusion | flops 4331665408 | bytes 29376512 | tf_op jit(solution)/shard_map/dot_general | solution.py:28
  254.1 8.0 %convolution_convert_fusion.2 = bf16[1024,1024]{1,0:T(8,128)(2,1)} fusion(bf16[1024,2048]{1,0:T(8,128)(2,1)} %get-tuple-element.285, bf16[1024,2048]{1,0:T(8,128)(2,1)S(1)} %copy-done.37), kind=kOutput, calls=%fused_computation.118 | convolution fusion | flops 4296015872 | bytes 10485760 | tf_op jit(solution)/shard_map/dot_general | solution.py:28
  262.2 63.0 %all-reduce.12.cloned.1.call-done = bf16[1024,1024]{1,0:T(8,128)(2,1)} async-done(((bf16[1024,1024]{1,0:T(8,128)(2,1)}), bf16[1024,1024]{1,0:T(8,128)(2,1)}) %all-reduce.12.cloned.1.call-update) | async-done | bytes 2097168 | tf_op jit(solution)/shard_map/psum | solution.py:149
  325.2 5.7 multiply_reduce_fusion.1
  337.9 3.9 reshape.153
  341.8 3.3 copy.77
  346.2 42.9 %while.27 = (s32[]{:T(128)}, bf16[2,512,512]{1,2,0:T(8,128)(2,1)}, bf16[2,512,512]{2,1,0:T(8,128)(2,1)}, bf16[2,512,512]{1,2,0:T(8,128)(2,1)}, bf16[2,512,8,64]{...) while((s32[]{:T(128)}, bf16[2,512,512]{1,2,0:T(8,128)(2,1)}, ...), condition=%wide.region_17.18_spmd, body=%wide.region_15.17_spmd.sunk | while | flops 1374941184 | bytes 89248512 | solution.py:160
  346.2 2.6 fusion.126
  348.8 2.9 fusion.127
  351.8 3.0 multiply_reduce_fusion.7
  354.7 2.8 multiply_convert_fusion.3
  367.6 2.6 fusion.126
  370.2 2.9 fusion.127
  373.1 3.0 multiply_reduce_fusion.7
  376.1 2.8 multiply_convert_fusion.3
  393.7 7.7 convert_bitcast_fusion
  401.4 7.7 copy.83
  409.1 4.8 convolution_convert_fusion.5
  414.0 10.2 %convolution_convert_fusion = bf16[2048,1024]{0,1:T(8,128)(2,1)} fusion(bf16[1024,2048]{1,0:T(8,128)(2,1)} %copy-done.40, f32[1024,1024]{1,0:T(8,128)} %copy-done.11), kind=kOutput, calls=%fused_computation.91 | convolution fusion | flops 4298113024 | bytes 12582912 | tf_op jit(solution)/shard_map/dot_general | solution.py:22
  424.3 6.6 bitcast_convert_fusion
  431.3 10.2 %convolution_convert_fusion.1 = bf16[1024,2048]{1,0:T(8,128)(2,1)} fusion(bf16[1024,2048]{1,0:T(8,128)(2,1)} %get-tuple-element.285, f32[1024,1024]{1,0:T(8,128)} %copy-done.7, f32[1024]{0:T(1024)S(1)} %copy-done.25, f32[1024]{0:T(1024)S(1)} %convert_element_type.169), kind=kOutput, calls=%fused_computation.92 | convolution fusion | flops 4300210176 | bytes 12591104 | tf_op jit(solution)/shard_map/dot_general | solution.py:22
  445.8 3.6 convert_reduce_fusion.1
  452.0 68.8 %all-reduce.14.cloned.1.call-done = bf16[3,1024,512]{2,0,1:T(4,128)(2,1)} async-done(((bf16[3,1024,512]{2,0,1:T(4,128)(2,1)}), bf16[3,1024,512]{2,0,1:T(4,128)(2,1)}) %all-reduce.14.cloned.1.call-update) | async-done | bytes 3145744
  522.7 57.9 %reduce-scatter.7.cloned.1.call-done = bf16[512,64]{0,1:T(8,128)(2,1)} async-done(((bf16[512,1024]{0,1:T(8,128)(2,1)}), bf16[512,64]{0,1:T(8,128)(2,1)}) %reduce-scatter.7.cloned.1.call-update) | async-done | bytes 65552 | tf_op jit(solution)/shard_map/reduce_scatter | solution.py:185
  582.1 74.2 %reduce-scatter.11.cloned.1.call-done = bf16[2048,64]{0,1:T(8,128)(2,1)} async-done(((bf16[2048,1024]{0,1:T(8,128)(2,1)}), bf16[2048,64]{0,1:T(8,128)(2,1)}) %reduce-scatter.11.cloned.1.call-update) | async-done | bytes 262160 | tf_op jit(solution)/shard_map/reduce_scatter | solution.py:191
  658.1 31.3 %reduce-scatter.5.cloned.1.call-done = bf16[512,1024]{1,0:T(8,128)(2,1)} async-done(((bf16[1024,1024]{1,0:T(8,128)(2,1)}), bf16[512,1024]{1,0:T(8,128)(2,1)}) %reduce-scatter.5.cloned.1.call-update) | async-done | bytes 1048592 | tf_op jit(solution)/shard_map/reduce_scatter | solution.py:179
  689.4 3.2 dynamic-slice_reduce_fusion.4
  692.6 62.3 %all-reduce.1 = (f32[2,1024]{1,0:T(2,128)S(1)}, f32[1024]{0:T(1024)S(1)}, f32[1024]{0:T(1024)S(1)}, f32[1024]{0:T(1024)S(1)}, f32[4096]{0:T(1024)S(1)}, /*index=...) all-reduce(f32[2,1024]{1,0:T(2,128)S(1)} %maximum_dynamic-update-sl, ...), channel_id=1, replica_groups=mesh['dp'=16,'mp'=2] {'dp'}, use_global_device_ids=true, to_apply=%region_22.23 | all-reduce | flops 12288 | bytes 98304 | tf_op jit(solution)/shard_map/psum | solution.py:202
  754.9 8.3 %all-reduce.2 = (f32[2,1024]{1,0:T(2,128)}, f32[1024]{0:T(1024)}, f32[1024]{0:T(1024)}, f32[1024]{0:T(1024)}, f32[4096]{0:T(1024)}, /*index=5*/f32[1024]{0:T(1024)}, f32[1024]{0:T(1024)}, f32[1024]{0:T(1024)}) all-reduce(f32[2,1024]{1,0:T(2,128)S(1)} %get-tuple-element.244, ...), channel_id=1, replica_groups=mesh['dp'=16,'mp'=2] {'mp'}, use_global_device_ids=true, to_apply=%region_23.24 | all-reduce | flops 12288 | bytes 98304 | tf_op jit(solution)/shard_map/psum | solution.py:201
  763.2 3.5 reduce-scatter.9.cloned.1.call-done
  (181 shorter events, 78.7 us)
Async XLA Ops:
  7.2 119.5 %all-reduce.8.cloned.1.call-start = ((), (), s32[]{:S(2)}) async-start(), calls=%async_computation.4 | async-start | bytes 4194304 | tf_op jit(solution)/shard_map/psum | solution.py:119
  35.6 2.0 copy-start.15
  56.7 4.5 copy-start.28
  56.7 4.5 copy-start.29
  56.7 4.5 copy-start.30
  56.7 4.6 copy-start.27
  60.9 167.8 %all-reduce.10.cloned.1.call-start = ((), (), s32[]{:S(2)}) async-start(), calls=%async_computation.5 | async-start | bytes 4194304 | tf_op jit(solution)/shard_map/psum | solution.py:132
  61.3 171.4 %copy-start.24 = (f32[1024]{0:T(1024)}, f32[1024]{0:T(1024)S(1)}, u32[]{:S(2)}) copy-start(f32[1024]{0:T(1024)S(1)} %convert_element_type.170) | copy-start | bytes 12292
  126.7 3.1 copy-start.3
  126.7 3.5 copy-start.5
  131.3 2.2 copy-start.36
  133.4 24.4 %copy-start.7 = (f32[1024,1024]{1,0:T(8,128)}, f32[1024,1024]{1,0:T(8,128)S(1)}, u32[]{:S(2)}) copy-start(f32[1024,1024]{1,0:T(8,128)S(1)} %broadcast_multiply_fusion) | copy-start | bytes 12582916
  133.5 26.5 %copy-start.34 = (bf16[2048,1024]{1,0:T(8,128)(2,1)S(1)}, bf16[2048,1024]{1,0:T(8,128)(2,1)}, u32[]{:S(2)}) copy-start(bf16[2048,1024]{1,0:T(8,128)(2,1)} %param.29) | copy-start | bytes 12582916
  157.9 2.0 copy-start.40
  159.9 6.2 copy-start.31
  159.9 6.2 copy-start.32
  165.7 159.5 %all-reduce.12.cloned.1.call-start = ((), (), s32[]{:S(2)}) async-start(), calls=%async_computation.6 | async-start | bytes 4194304 | tf_op jit(solution)/shard_map/psum | solution.py:149
  166.2 72.0 %copy-start.20 = (f32[1024]{0:T(1024)}, f32[1024]{0:T(1024)S(1)}, u32[]{:S(2)}) copy-start(f32[1024]{0:T(1024)S(1)} %convert_element_type.177) | copy-start | bytes 12292
  228.8 4.0 copy-start.8
  228.8 4.7 copy-start.13
  237.0 2.4 copy-start.10
  237.0 2.4 copy-start.22
  238.2 3.0 copy-start.35
  239.4 14.7 %copy-start.11 = (f32[1024,1024]{1,0:T(8,128)}, f32[1024,1024]{1,0:T(8,128)S(1)}, u32[]{:S(2)}) copy-start(f32[1024,1024]{1,0:T(8,128)S(1)} %broadcast_add_fusion.1) | copy-start | bytes 12582916
  241.1 13.0 %copy-start.37 = (bf16[1024,2048]{1,0:T(8,128)(2,1)S(1)}, bf16[1024,2048]{1,0:T(8,128)(2,1)}, u32[]{:S(2)}) copy-start(bf16[1024,2048]{1,0:T(8,128)(2,1)} %param.27) | copy-start | bytes 12582916
  262.1 258.7 %all-reduce.14.cloned.1.call-start = ((), (), s32[]{:S(2)}) async-start(), calls=%async_computation.11 | async-start | bytes 8388608
  325.2 5.8 copy-start.4
  325.2 5.8 copy-start.6
  330.9 2.4 copy-start.12
  333.4 2.3 copy-start.38
  346.2 2.6 copy-start.14
  348.8 2.9 copy-start.16
  354.7 2.9 copy-start.2
  357.6 2.2 copy-start.1
  367.6 2.6 copy-start.14
  370.2 2.9 copy-start.16
  376.1 2.9 copy-start.2
  379.0 2.2 copy-start.1
  409.1 171.5 %reduce-scatter.7.cloned.1.call-start = ((), (), s32[]{:S(2)}) async-start(), calls=%async_computation.8 | async-start | bytes 1114112 | tf_op jit(solution)/shard_map/reduce_scatter | solution.py:185
  414.0 242.3 %reduce-scatter.11.cloned.1.call-start = ((), (), s32[]{:S(2)}) async-start(), calls=%async_computation.10 | async-start | bytes 4456448 | tf_op jit(solution)/shard_map/reduce_scatter | solution.py:191
  424.3 7.0 copy-start.25
  424.3 265.1 %reduce-scatter.5.cloned.1.call-start = ((), (), s32[]{:S(2)}) async-start(), calls=%async_computation.7 | async-start | bytes 3145728 | tf_op jit(solution)/shard_map/reduce_scatter | solution.py:179
  431.0 335.8 %reduce-scatter.9.cloned.1.call-start = ((), (), s32[]{:S(2)}) async-start(), calls=%async_computation.9 | async-start | bytes 4456448 | tf_op jit(solution)/shard_map/reduce_scatter | solution.py:188
  441.5 2.0 copy-start.26
  441.5 4.3 copy-start.21
  443.4 6.0 copy-start.9
  445.8 5.8 copy-start.18
  445.8 5.8 copy-start.19
  (6 other events, 9.1 us)
Sparse Core Ops, SparseCore 0:
  61.1 65.5 all-reduce.7
  165.8 62.9 all-reduce.9
  262.2 62.9 all-reduce.11
  409.2 111.5 all-reduce.13
  524.3 56.2 reduce-scatter.6
  584.8 71.4 reduce-scatter.10
  658.5 30.8 reduce-scatter.4
  693.8 72.9 reduce-scatter.8
